TPU v7x, 32 devices: a whole 2x2x4 slice. The times are simulated.
32 devices in a mesh: orb: 2 (over x), grid: 16 (over z, y, core).
Axes of the slice: x: 2, y: 2, z: 4, core: 2. Of those that a mesh axis runs over, the one named last changes fastest.
Arguments:
- orbitals: bfloat16 [2, 1024, 2304], P('orb', 'grid'), may hold values from -6 to 6
- continuum: bfloat16 [4, 1024, 2304], P(None, 'grid'), may hold values from -6 to 6
- harmonic_table: bfloat16 [2560, 2304], P('orb'), may hold values from -0.125 to 0.125
- ang_weight: float32 [2560], P('orb'), may hold values from 0.5 to 2
- channel_lm: int32 [2304], replicated, may hold values from 0 to 2303, each once
Outputs:
- exchange_out: float32 [2304, 4, 1024], P('orb', None, 'grid')
Inputs may be any that keep to these rules, and one draw needn't show every extreme that they name: channel_lm names each harmonic index lm = l * l + l + m (l up to 47) exactly once.
All inputs are finite; a program needn't handle non-finite values.
Results may differ from a plain program's by a relative error of at most 0.03.
Values may be sent and summed in bfloat16 or wider, within the bound.
No kernel may reach another device: no remote copies, remote signals or barrier semaphores. Data moves between devices by JAX's collectives and lax.ppermute only.
A program may use at most 128 MiB of HBM per device.

v0:
```python
import math
import jax
import jax.numpy as jnp
from jax import lax
from jax.sharding import PartitionSpec as P

LMAX = 47
LM = 2304
LOG_SPAN = 7.0


def combine(earlier, later):
    return (earlier[0] * later[0], earlier[1] * later[0] + later[1])


def channel_degree(lm_index):
    levels = jnp.arange(1, LMAX + 1, dtype=jnp.int32)
    return jnp.sum((lm_index[:, None] >= levels * levels).astype(jnp.float32), axis=1)


def line_sums(forward_source, backward_source, decay_rate, block_size):
    lead_first, lead_second, count, channels = forward_source.shape
    block_count = count // block_size
    forward_blocks = forward_source.reshape(
        lead_first, lead_second, block_count, block_size, channels
    )
    backward_blocks = backward_source.reshape(
        lead_first, lead_second, block_count, block_size, channels
    )
    forward = forward_blocks
    backward = backward_blocks
    for distance in range(1, block_size):
        factor = jnp.exp(-decay_rate * distance)
        padding = jnp.zeros((lead_first, lead_second, block_count, distance, channels), jnp.float32)
        forward = forward + factor * jnp.concatenate(
            [padding, forward_blocks[:, :, :, : block_size - distance]], axis=3
        )
        backward = backward + factor * jnp.concatenate(
            [backward_blocks[:, :, :, distance:], padding], axis=3
        )
    block_decay = jnp.broadcast_to(
        jnp.exp(-decay_rate * block_size), (lead_first, lead_second, block_count, channels)
    )
    forward_total = lax.associative_scan(
        combine, (block_decay, forward[:, :, :, block_size - 1]), axis=2
    )[1]
    backward_total = lax.associative_scan(
        combine, (block_decay, backward[:, :, :, 0]), reverse=True, axis=2
    )[1]
    boundary = jnp.zeros((lead_first, lead_second, 1, channels), jnp.float32)
    earlier_sum = jnp.concatenate([boundary, forward_total[:, :, : block_count - 1]], axis=2)
    later_sum = jnp.concatenate([backward_total[:, :, 1:], boundary], axis=2)
    offsets = jnp.arange(block_size, dtype=jnp.float32)[:, None]
    forward = forward + jnp.exp(-decay_rate * (offsets + 1.0)) * earlier_sum[:, :, :, None, :]
    backward = (
        backward + jnp.exp(-decay_rate * (block_size - offsets)) * later_sum[:, :, :, None, :]
    )
    shape = forward_source.shape
    return (
        forward.reshape(shape),
        backward.reshape(shape),
        forward_total[:, :, block_count - 1],
        backward_total[:, :, 0],
    )


def local_lines(density, degree, points):
    count = density.shape[2]
    increment = LOG_SPAN / points
    positions = jnp.arange(count, dtype=jnp.int32).astype(jnp.float32)[:, None]
    radius = jnp.exp((positions + 1.0 - points) * increment)
    decay_rate = degree * increment
    source = increment * radius * density
    scaled = increment * density
    forward, backward, forward_end, backward_end = line_sums(
        source, scaled, decay_rate, math.gcd(count, 16)
    )
    return (forward, backward, forward_end, backward_end, radius, scaled, decay_rate)


def finish_potential(forward, backward, radius, scaled, degree):
    factor = 4.0 / (2.0 * degree + 1.0)
    return factor * (forward / radius + backward - scaled)


def shards(orbitals, continuum, harmonic_table, ang_weight, channel_lm):
    analysis = (ang_weight[:, None] * harmonic_table.astype(jnp.float32)).astype(jnp.bfloat16)
    phi_ang = jnp.einsum(
        "al,irl->ira",
        harmonic_table,
        lax.all_gather(orbitals, "orb", axis=0, tiled=True),
        preferred_element_type=jnp.float32,
    ).astype(jnp.bfloat16)
    continuum_angular = jnp.einsum(
        "al,krl->kra", harmonic_table, continuum, preferred_element_type=jnp.float32
    ).astype(jnp.bfloat16)
    pair_values = (
        phi_ang.astype(jnp.float32)[:, None] * continuum_angular.astype(jnp.float32)[None]
    ).astype(jnp.bfloat16)
    density = lax.psum_scatter(
        jnp.einsum(
            "al,ikra->ikrl", analysis, pair_values, preferred_element_type=jnp.float32
        ).astype(jnp.bfloat16),
        "orb",
        scatter_dimension=0,
        tiled=True,
    )
    local_count = LM // lax.axis_size("grid")
    local_channel_index = lax.dynamic_slice_in_dim(
        channel_lm, lax.axis_index("grid") * local_count, local_count
    )
    degree = channel_degree(local_channel_index)
    line_density = lax.all_to_all(density, "grid", split_axis=3, concat_axis=2, tiled=True)
    points = line_density.shape[2]
    forward, backward, forward_end, backward_end, radius, scaled, decay_rate = local_lines(
        line_density.astype(jnp.float32), degree, points
    )
    potential = finish_potential(forward, backward, radius, scaled, degree).astype(jnp.bfloat16)
    radial_potential = lax.all_to_all(potential, "grid", split_axis=2, concat_axis=3, tiled=True)
    pot_ang = jnp.einsum(
        "al,ikrl->ikra",
        harmonic_table,
        lax.all_gather(radial_potential, "orb", axis=0, tiled=True),
        preferred_element_type=jnp.float32,
    )
    weighted_values = jnp.sum(phi_ang.astype(jnp.float32)[:, None] * pot_ang, axis=0)
    product = weighted_values.astype(jnp.bfloat16)
    return -lax.psum_scatter(
        jnp.einsum("al,kra->lkr", analysis, product, preferred_element_type=jnp.float32),
        "orb",
        scatter_dimension=0,
        tiled=True,
    )


def solution(mesh):
    return jax.shard_map(
        shards,
        mesh=mesh,
        in_specs=(P("orb", "grid", None), P(None, "grid", None), P("orb", None), P("orb"), P()),
        out_specs=P("orb", None, "grid"),
        check_vma=False,
    )
```

profile of v0, /device:TPU:0, one launch (start us, length us, event | category | flops | bytes accessed | tf_op | source)
XLA Modules:
  0.0 537.0 jit_solution(362612435213121791)
XLA Ops:
  6.5 11.0 %all_gather.6 = bf16[2,64,2304]{2,1,0:T(8,128)(2,1)S(1)} all-gather(bf16[1,64,2304]{2,1,0:T(8,128)(2,1)} %param.5), channel_id=1, replica_groups=mesh['orb'=2,'grid'=16] {'orb'}, dimensions={0}, use_global_device_ids=true | all-gather | bytes 884736 | tf_op jit(solution)/shard_map/all_gather | solution.py:91
  17.5 4.8 fusion.27
  24.1 5.0 fusion.10
  29.2 36.4 %reduce-scatter.3.cloned.1.call-done = bf16[1,4,64,2304]{3,2,1,0:T(8,128)(2,1)} async-done(((bf16[2,4,64,2304]{3,2,1,0:T(8,128)(2,1)}), bf16[1,4,64,2304]{3,2,1,0:T(8,128)(2,1)}) %reduce-scatter.3.cloned.1.call-update) | async-done | bytes 1179664 | tf_op jit(solution)/shard_map/reduce_scatter | solution.py:100
  65.5 4.2 copy.104
  72.2 5.6 %all-to-all-start = ((bf16[16,2,18432]{2,1,0:T(2,128)(2,1)}), bf16[16,2,18432]{2,1,0:T(2,128)(2,1)S(1)}, u32[]{:S(2)}, u32[]{:S(2)}) async-start(bf16[16,2,18432]{2,1,0:T(2,128)(2,1)} %reshape.319), calls=%async_computation.1 | async-start | bytes 2359296 | tf_op jit(solution)/shard_map/all_to_all | solution.py:113
  81.4 21.5 %all-to-all-done = bf16[16,2,18432]{2,1,0:T(2,128)(2,1)S(1)} async-done(((bf16[16,2,18432]{2,1,0:T(2,128)(2,1)}), bf16[16,2,18432]{2,1,0:T(2,128)(2,1)S(1)}, u32[]{:S(2)}, u32[]{:S(2)}) %all-to-all-start) | async-done | bytes 1179680 | tf_op jit(solution)/shard_map/all_to_all | solution.py:113
  104.5 5.4 %copy.132 = f32[1,4,64,16,144]{4,2,3,1,0:T(8,128)} copy(bf16[1,4,64,16,144]{2,1,4,3,0:T(4,128)(2,1)S(1)} %bitcast.77) | data formatting | bytes 3538944 | tf_op jit(solution)/shard_map/convert_element_type | solution.py:116
  109.8 7.8 %copy_multiply_fusion = f32[1,4,64,16,144]{4,0,3,2,1:T(1,128)S(1)} fusion(f32[1,4,64,16,144]{4,3,2,1,0:T(8,128)} %bitcast.74, f32[64,16]{1,0:T(8,128)S(1)} %copy-done.29), kind=kLoop, calls=%fused_computation.17 | loop fusion | flops 589824 | bytes 4722688 | tf_op jit(solution)/shard_map/mul | solution.py:73
  117.7 5.5 %slice.492 = f32[1,4,64,15,144]{4,0,3,2,1:T(1,128)} slice(f32[1,4,64,16,144]{4,0,3,2,1:T(1,128)S(1)} %copy_multiply_fusion), slice={[0:1], [0:4], [0:64], [0:15], [0:144]} | slice | bytes 4423680 | tf_op jit(solution)/shard_map/slice | solution.py:36
  123.1 5.2 slice.493
  128.4 3.1 slice.494
  131.4 3.0 slice.495
  134.5 2.6 slice.496
  143.5 3.2 slice.500
  146.7 2.6 slice.501
  154.5 43.8 %multiply_add_fusion.3 = f32[1,4,64,16,144]{4,0,3,2,1:T(1,128)S(1)} fusion(f32[1,4,64,1,144]{4,0,3,2,1:T(1,128)S(1)} %slice.506, f32[1,4,64,2,144]{4,0,3,2,1:T(1,128)S(1)} %slice.505, f32[1,4,64,3,144]{4,0,3,2,1:T(1,128)S(1)} %slice.504, f32[1,4,64,4,144]{4,0,3,2,1:T(1,128)S(1)} %slice.503, f32[1,4,64,5,144]{4,0,3,2,1:T(1,128)} %slice.502, ...), kind=kLoop, calls=%fused_computation.21 | loop fusion | flops 18284544 | bytes 22426048 | tf_op jit(solution)/shard_map/add | solution.py:35
  206.0 2.7 broadcast_multiply_fusion.1
  208.7 3.0 slice.526
  211.7 2.6 slice.527
  214.3 2.7 slice.528
  217.0 2.6 slice.529
  219.6 2.6 slice.530
  222.2 2.6 slice.531
  224.8 2.7 slice.532
  235.9 8.1 %copy.157 = f32[1,4,64,15,144]{4,0,3,2,1:T(1,128)} copy(f32[1,4,64,15,144]{4,3,2,1,0:T(8,128)} %slice.526) | data formatting | bytes 4423680
  244.0 8.1 %copy.156 = f32[1,4,64,14,144]{4,0,3,2,1:T(1,128)} copy(f32[1,4,64,14,144]{4,3,2,1,0:T(8,128)} %slice.527) | data formatting | bytes 4128768
  252.2 5.4 %copy.155 = f32[1,4,64,13,144]{4,0,3,2,1:T(1,128)} copy(f32[1,4,64,13,144]{4,3,2,1,0:T(8,128)S(1)} %copy-done.10) | data formatting | bytes 3833856
  257.6 3.3 copy.154
  260.9 4.8 copy.153
  265.7 2.8 copy.152
  268.5 2.5 copy.151
  273.2 4.8 copy.149
  278.1 3.2 copy.148
  281.4 3.1 copy.147
  288.4 35.6 %multiply_add_fusion.1 = f32[1,4,64,16,144]{4,0,3,2,1:T(1,128)S(1)} fusion(f32[1,4,64,2,144]{4,0,3,2,1:T(1,128)S(1)} %copy.144, f32[1,4,64,3,144]{4,0,3,2,1:T(1,128)S(1)} %copy.145, f32[1,4,64,4,144]{4,0,3,2,1:T(1,128)S(1)} %copy.146, f32[1,4,64,5,144]{4,0,3,2,1:T(1,128)S(1)} %copy.147, f32[1,4,64,6,144]{4,0,3,2,1:T(1,128)} %copy.148, ...), kind=kLoop, calls=%fused_computation.19 | loop fusion | flops 16515072 | bytes 22273920 | tf_op jit(solution)/shard_map/add | solution.py:38
  331.0 10.6 %pad.124 = f32[1,4,16,144]{3,0,2,1:T(1,128)S(1)} pad(f32[1,4,8,144]{3,0,2,1:T(1,128)} %pad_maximum_fusion.5, f32[]{:T(128)} %constant.31.clone.1), padding=0_0_0x0_0_0x0_1_1x0_0_0 | pad | bytes 55300 | tf_op jit(solution)/shard_map/pad | solution.py:47
  342.5 3.0 broadcast_multiply_fusion
  349.5 9.2 %multiply_add_fusion.2 = f32[1,4,64,16,144]{4,0,3,2,1:T(1,128)} fusion(f32[1,4,64,16,144]{4,0,3,2,1:T(1,128)} %copy-done.6, f32[4,64,144]{2,1,0:T(8,128)S(1)} %pad_bitcast_fusion.1, f32[16,144]{1,0:T(8,128)S(1)} %copy-done.31), kind=kLoop, calls=%fused_computation.20 | loop fusion | flops 1179648 | bytes 4875264 | tf_op jit(solution)/shard_map/add | solution.py:54
  358.7 4.7 copy.136
  369.5 7.0 %copy.134 = f32[1,4,64,16,144]{4,2,3,1,0:T(8,128)} copy(f32[1,4,64,16,144]{2,1,4,3,0:T(4,128)} %bitcast.78) | data formatting | bytes 4718592 | tf_op jit(solution)/shard_map/mul | solution.py:74
  376.5 3.1 multiply_add_fusion
  384.5 54.8 %all_to_all.27 = bf16[1,4,1024,144]{3,1,0,2:T(4,128)(2,1)S(1)} all-to-all(bf16[1,4,1024,144]{3,1,0,2:T(4,128)(2,1)S(1)} %copy.127), channel_id=1, replica_groups=mesh['orb'=2,'grid'=16] {'grid'}, dimensions={2} | all-to-all | bytes 2359296 | tf_op jit(solution)/shard_map/all_to_all | solution.py:119
  440.5 4.1 all_to_all.24
  444.6 35.6 %all-gather.2.cloned.1.call-done = bf16[2,4,64,2304]{3,2,1,0:T(8,128)(2,1)} async-done(((bf16[1,4,64,2304]{3,2,1,0:T(8,128)(2,1)}), bf16[2,4,64,2304]{3,2,1,0:T(8,128)(2,1)}) %all-gather.2.cloned.1.call-update) | async-done | bytes 2359312 | tf_op jit(solution)/shard_map/all_gather | solution.py:123
  480.3 6.7 %fusion.30 = bf16[4,64,1280]{2,1,0:T(8,128)(2,1)S(1)} fusion(bf16[2,4,64,2304]{3,2,1,0:T(8,128)(2,1)} %all-gather.2.cloned.1.call-done, bf16[1280,2304]{1,0:T(8,128)(2,1)} %param.7, f32[2,64,1280]{2,1,0:T(8,128)S(1)} %copy-done.27), kind=kOutput, calls=%fused_computation.31 | convolution fusion | flops 3020881920 | bytes 9568256 | tf_op jit(solution)/shard_map/al,ikrl->ikra/dot_general | solution.py:120
  487.0 6.0 %fusion.8 = f32[2304,4,64]{0,2,1:T(8,128)} fusion(bf16[1280,2304]{1,0:T(8,128)(2,1)} %param.7, f32[1280]{0:T(1024)S(1)} %copy-done.75, bf16[4,64,1280]{2,1,0:T(8,128)(2,1)S(1)} %fusion.30), kind=kOutput, calls=%fused_computation.9 | convolution fusion | flops 1518796800 | bytes 8918016 | tf_op jit(solution)/shard_map/al,kra->lkr/dot_general | solution.py:129
  493.0 34.9 %reduce-scatter.5.cloned.1.call-done = f32[1152,4,64]{0,2,1:T(8,128)} async-done(((f32[2304,4,64]{0,2,1:T(8,128)}), f32[1152,4,64]{0,2,1:T(8,128)}) %reduce-scatter.5.cloned.1.call-update) | async-done | bytes 1179664 | tf_op jit(solution)/shard_map/reduce_scatter | solution.py:128
  (285 shorter events, 68.5 us)
Async XLA Ops:
  6.5 15.8 %copy-start = (bf16[4,64,2304]{2,1,0:T(8,128)(2,1)S(1)}, bf16[4,64,2304]{2,1,0:T(8,128)(2,1)}, u32[]{:S(2)}) copy-start(bf16[4,64,2304]{2,1,0:T(8,128)(2,1)} %param.6) | copy-start | bytes 3538948
  6.5 59.0 %reduce-scatter.3.cloned.1.call-start = ((), (), s32[]{:S(2)}) async-start(), calls=%async_computation.4 | async-start | bytes 3538944 | tf_op jit(solution)/shard_map/reduce_scatter | solution.py:100
  6.5 15.8 %slice-start.1 = ((s8[5898240]{0:T(1024)(128)(4,1)}), s8[4194304]{0:T(1024)(128)(4,1)S(1)}, s32[]{:S(2)}) async-start(s8[5898240]{0:T(1024)(128)(4,1)} %bitcast.80), calls=%async_computation.8 | async-start | bytes 8388608
  72.2 30.8 %all-to-all-start = ((bf16[16,2,18432]{2,1,0:T(2,128)(2,1)}), bf16[16,2,18432]{2,1,0:T(2,128)(2,1)S(1)}, u32[]{:S(2)}, u32[]{:S(2)}) async-start(bf16[16,2,18432]{2,1,0:T(2,128)(2,1)} %reshape.319), calls=%async_computation.1 | async-start | bytes 2359296 | tf_op jit(solution)/shard_map/all_to_all | solution.py:113
  77.8 402.5 %all-gather.2.cloned.1.call-start = ((), (), s32[]{:S(2)}) async-start(), calls=%async_computation.5 | async-start | bytes 3538944 | tf_op jit(solution)/shard_map/all_gather | solution.py:123
  143.5 10.7 %copy-start.16 = (f32[1,4,64,14,144]{4,0,3,2,1:T(1,128)S(1)}, f32[1,4,64,14,144]{4,0,3,2,1:T(1,128)}, u32[]{:S(2)}) copy-start(f32[1,4,64,14,144]{4,0,3,2,1:T(1,128)} %slice.493) | copy-start | bytes 6193156
  146.7 7.5 %copy-start.15 = (f32[1,4,64,15,144]{4,0,3,2,1:T(1,128)S(1)}, f32[1,4,64,15,144]{4,0,3,2,1:T(1,128)}, u32[]{:S(2)}) copy-start(f32[1,4,64,15,144]{4,0,3,2,1:T(1,128)} %slice.492) | copy-start | bytes 6635524
  154.4 46.2 %copy-start.32 = (f32[144]{0:T(256)S(1)}, f32[144]{0:T(256)}, u32[]{:S(2)}) copy-start(f32[144]{0:T(256)} %get-tuple-element.42) | copy-start | bytes 1732
  154.4 46.3 %copy-start.68 = (f32[144]{0:T(256)S(1)}, f32[144]{0:T(256)}, u32[]{:S(2)}) copy-start(f32[144]{0:T(256)} %get-tuple-element.43) | copy-start | bytes 1732
  154.4 46.4 %copy-start.69 = (f32[144]{0:T(256)S(1)}, f32[144]{0:T(256)}, u32[]{:S(2)}) copy-start(f32[144]{0:T(256)} %get-tuple-element.47) | copy-start | bytes 1732
  154.4 46.5 %copy-start.70 = (f32[144]{0:T(256)S(1)}, f32[144]{0:T(256)}, u32[]{:S(2)}) copy-start(f32[144]{0:T(256)} %get-tuple-element.46) | copy-start | bytes 1732
  154.4 46.5 %copy-start.71 = (f32[144]{0:T(256)S(1)}, f32[144]{0:T(256)}, u32[]{:S(2)}) copy-start(f32[144]{0:T(256)} %get-tuple-element.44) | copy-start | bytes 1732
  154.4 46.5 %copy-start.73 = (f32[144]{0:T(256)S(1)}, f32[144]{0:T(256)}, u32[]{:S(2)}) copy-start(f32[144]{0:T(256)} %get-tuple-element.45) | copy-start | bytes 1732
  200.6 8.1 %copy-start.25 = (f32[1,4,64,144]{3,0,2,1:T(1,128)}, f32[1,4,64,144]{3,0,2,1:T(1,128)S(1)}, u32[]{:S(2)}) copy-start(f32[1,4,64,144]{3,0,2,1:T(1,128)S(1)} %slice_bitcast_fusion.1) | copy-start | bytes 442372
  208.7 26.2 %copy-start.2 = (f32[1,4,64,16,144]{4,3,2,1,0:T(8,128)}, f32[1,4,64,16,144]{4,3,2,1,0:T(8,128)S(1)}, u32[]{:S(2)}) copy-start(f32[1,4,64,16,144]{4,3,2,1,0:T(8,128)S(1)} %broadcast_multiply_fusion.1) | copy-start | bytes 7077892
  244.0 8.1 %copy-start.10 = (f32[1,4,64,13,144]{4,3,2,1,0:T(8,128)S(1)}, f32[1,4,64,13,144]{4,3,2,1,0:T(8,128)}, u32[]{:S(2)}) copy-start(f32[1,4,64,13,144]{4,3,2,1,0:T(8,128)} %slice.528) | copy-start | bytes 5750788
  268.5 9.6 %copy-start.20 = (f32[1,4,64,6,144]{4,3,2,1,0:T(8,128)S(1)}, f32[1,4,64,6,144]{4,3,2,1,0:T(8,128)}, u32[]{:S(2)}) copy-start(f32[1,4,64,6,144]{4,3,2,1,0:T(8,128)} %slice.535) | copy-start | bytes 2654212
  271.0 17.1 %copy-start.19 = (f32[1,4,64,11,144]{4,0,3,2,1:T(1,128)S(1)}, f32[1,4,64,11,144]{4,0,3,2,1:T(1,128)}, u32[]{:S(2)}) copy-start(f32[1,4,64,11,144]{4,0,3,2,1:T(1,128)} %copy.153) | copy-start | bytes 4866052
  273.2 14.4 %copy-start.23 = (f32[1,4,64,2,144]{4,3,2,1,0:T(2,128)S(1)}, f32[1,4,64,2,144]{4,3,2,1,0:T(2,128)}, u32[]{:S(2)}) copy-start(f32[1,4,64,2,144]{4,3,2,1,0:T(2,128)} %slice.539) | copy-start | bytes 884740
  273.2 15.0 %copy-start.18 = (f32[1,4,64,13,144]{4,0,3,2,1:T(1,128)S(1)}, f32[1,4,64,13,144]{4,0,3,2,1:T(1,128)}, u32[]{:S(2)}) copy-start(f32[1,4,64,13,144]{4,0,3,2,1:T(1,128)} %copy.155) | copy-start | bytes 5750788
  278.1 10.1 %copy-start.17 = (f32[1,4,64,14,144]{4,0,3,2,1:T(1,128)S(1)}, f32[1,4,64,14,144]{4,0,3,2,1:T(1,128)}, u32[]{:S(2)}) copy-start(f32[1,4,64,14,144]{4,0,3,2,1:T(1,128)} %copy.156) | copy-start | bytes 6193156
  281.3 6.9 %copy-start.14 = (f32[1,4,64,15,144]{4,0,3,2,1:T(1,128)S(1)}, f32[1,4,64,15,144]{4,0,3,2,1:T(1,128)}, u32[]{:S(2)}) copy-start(f32[1,4,64,15,144]{4,0,3,2,1:T(1,128)} %copy.157) | copy-start | bytes 6635524
  281.3 7.0 %copy-start.41 = (f32[144]{0:T(256)S(1)}, f32[144]{0:T(256)}, u32[]{:S(2)}) copy-start(f32[144]{0:T(256)} %get-tuple-element.27) | copy-start | bytes 1732
  281.3 7.0 %copy-start.43 = (f32[144]{0:T(256)S(1)}, f32[144]{0:T(256)}, u32[]{:S(2)}) copy-start(f32[144]{0:T(256)} %get-tuple-element.28) | copy-start | bytes 1732
  281.3 7.0 %copy-start.45 = (f32[144]{0:T(256)S(1)}, f32[144]{0:T(256)}, u32[]{:S(2)}) copy-start(f32[144]{0:T(256)} %get-tuple-element.29) | copy-start | bytes 1732
  281.3 7.0 %copy-start.47 = (f32[144]{0:T(256)S(1)}, f32[144]{0:T(256)}, u32[]{:S(2)}) copy-start(f32[144]{0:T(256)} %get-tuple-element.30) | copy-start | bytes 1732
  281.3 7.0 %copy-start.49 = (f32[144]{0:T(256)S(1)}, f32[144]{0:T(256)}, u32[]{:S(2)}) copy-start(f32[144]{0:T(256)} %get-tuple-element.31) | copy-start | bytes 1732
  281.3 7.0 %copy-start.51 = (f32[144]{0:T(256)S(1)}, f32[144]{0:T(256)}, u32[]{:S(2)}) copy-start(f32[144]{0:T(256)} %get-tuple-element.32) | copy-start | bytes 1732
  281.3 7.0 %copy-start.53 = (f32[144]{0:T(256)S(1)}, f32[144]{0:T(256)}, u32[]{:S(2)}) copy-start(f32[144]{0:T(256)} %get-tuple-element.33) | copy-start | bytes 1732
  281.3 7.0 %copy-start.55 = (f32[144]{0:T(256)S(1)}, f32[144]{0:T(256)}, u32[]{:S(2)}) copy-start(f32[144]{0:T(256)} %get-tuple-element.34) | copy-start | bytes 1732
  281.3 7.0 %copy-start.57 = (f32[144]{0:T(256)S(1)}, f32[144]{0:T(256)}, u32[]{:S(2)}) copy-start(f32[144]{0:T(256)} %get-tuple-element.35) | copy-start | bytes 1732
  281.3 7.0 %copy-start.59 = (f32[144]{0:T(256)S(1)}, f32[144]{0:T(256)}, u32[]{:S(2)}) copy-start(f32[144]{0:T(256)} %get-tuple-element.36) | copy-start | bytes 1732
  281.3 7.0 %copy-start.61 = (f32[144]{0:T(256)S(1)}, f32[144]{0:T(256)}, u32[]{:S(2)}) copy-start(f32[144]{0:T(256)} %get-tuple-element.37) | copy-start | bytes 1732
  281.4 7.0 %copy-start.63 = (f32[144]{0:T(256)S(1)}, f32[144]{0:T(256)}, u32[]{:S(2)}) copy-start(f32[144]{0:T(256)} %get-tuple-element.38) | copy-start | bytes 1732
  281.4 7.0 %copy-start.65 = (f32[144]{0:T(256)S(1)}, f32[144]{0:T(256)}, u32[]{:S(2)}) copy-start(f32[144]{0:T(256)} %get-tuple-element.39) | copy-start | bytes 1732
  281.4 7.0 %copy-start.67 = (f32[144]{0:T(256)S(1)}, f32[144]{0:T(256)}, u32[]{:S(2)}) copy-start(f32[144]{0:T(256)} %get-tuple-element.40) | copy-start | bytes 1732
  288.4 35.6 %copy-start.22 = (f32[1,4,64,1,144]{4,3,2,1,0:T(1,128)S(1)}, f32[1,4,64,1,144]{4,3,2,1,0:T(1,128)}, u32[]{:S(2)}) copy-start(f32[1,4,64,1,144]{4,3,2,1,0:T(1,128)} %slice.540) | copy-start | bytes 442372
  288.4 35.6 %copy-start.36 = (f32[144]{0:T(256)S(1)}, f32[144]{0:T(256)}, u32[]{:S(2)}) copy-start(f32[144]{0:T(256)} %get-tuple-element.41) | copy-start | bytes 1732
  326.3 19.3 %copy-start.24 = (f32[1,4,64,144]{3,0,2,1:T(1,128)}, f32[1,4,64,144]{3,0,2,1:T(1,128)S(1)}, u32[]{:S(2)}) copy-start(f32[1,4,64,144]{3,0,2,1:T(1,128)S(1)} %slice_bitcast_fusion) | copy-start | bytes 442372
  329.6 17.6 %slice-start.4 = ((f32[1,4,64,144]{3,0,2,1:T(1,128)}), f32[1,4,1,144]{3,0,2,1:T(1,128)S(1)}, s32[]{:S(2)}) async-start(f32[1,4,64,144]{3,0,2,1:T(1,128)} %copy-done.25), calls=%async_computation.11 | async-start | bytes 8192 | tf_op jit(solution)/shard_map/slice | solution.py:44
  329.6 17.6 %copy-start.28 = (f32[1,4,31,144]{3,0,2,1:T(1,128)S(1)}, f32[1,4,31,144]{3,0,2,1:T(1,128)}, u32[]{:S(2)}) copy-start(f32[1,4,31,144]{3,0,2,1:T(1,128)} %fusion.38) | copy-start | bytes 214276
  358.7 8.2 %copy-start.34 = (f32[144]{0:T(256)S(1)}, f32[144]{0:T(256)}, u32[]{:S(2)}) copy-start(f32[144]{0:T(256)} %get-tuple-element.42) | copy-start | bytes 1732
  358.7 8.5 %slice-start.3 = ((f32[1,4,64,144]{3,0,2,1:T(1,128)}), f32[1,4,1,144]{3,0,2,1:T(1,128)S(1)}, s32[]{:S(2)}) async-start(f32[1,4,64,144]{3,0,2,1:T(1,128)} %copy-done.24), calls=%async_computation.10 | async-start | bytes 8192 | tf_op jit(solution)/shard_map/slice | solution.py:47
  369.5 7.0 %copy-start.37 = (f32[144]{0:T(256)S(1)}, f32[144]{0:T(256)}, u32[]{:S(2)}) copy-start(f32[144]{0:T(256)} %get-tuple-element.41) | copy-start | bytes 1732
  439.3 41.0 %copy-start.27 = (f32[2,64,1280]{2,1,0:T(8,128)S(1)}, f32[2,64,1280]{2,1,0:T(8,128)}, u32[]{:S(2)}) copy-start(f32[2,64,1280]{2,1,0:T(8,128)} %copy-done.26) | copy-start | bytes 1966084
  444.6 42.4 %copy-start.75 = (f32[1280]{0:T(1024)S(1)}, f32[1280]{0:T(1024)}, u32[]{:S(2)}) copy-start(f32[1280]{0:T(1024)} %param.8) | copy-start | bytes 15364
  444.6 83.3 %reduce-scatter.5.cloned.1.call-start = ((), (), s32[]{:S(2)}) async-start(), calls=%async_computation.6 | async-start | bytes 3538944 | tf_op jit(solution)/shard_map/reduce_scatter | solution.py:128
  487.0 43.3 %copy-start.1 = (bf16[4,64,2304]{2,1,0:T(8,128)(2,1)S(1)}, bf16[4,64,2304]{2,1,0:T(8,128)(2,1)}, u32[]{:S(2)}) copy-start(bf16[4,64,2304]{2,1,0:T(8,128)(2,1)} %param.6) | copy-start | bytes 3538948
  (37 other events, 162.1 us)
Sparse Core Ops, SparseCore 0:
  29.3 36.1 reduce-scatter.2
  444.7 35.5 all-gather.1
  493.1 34.6 reduce-scatter.4
where the time goes:
time: 543 us; the launch traced here: 537 us
  local copies, waits for them, and re-layouts  180 us (33%)
  waiting for transfers between devices  128 us (24%)
  other arithmetic  118 us (22%)
  blocking collectives  65.8 us (12%)
  matrix products  24.2 us (4%)
  between operations  14.9 us (3%)
  starting transfers between devices  5.71 us (1%)
    unnamed x179, local copies, waits for them, and re-layouts  69.2 us
    all_to_all x1, blocking collectives, shards(): lax.all_to_all(potential, 'grid', split_axis=2, concat_axis=3, tiled=True)  54.8 us
    add x1, other arithmetic, line_sums(): forward + factor * jnp.concatenate([padding, forward_blocks[:, :, :, :blo...  43.8 us
    reduce_scatter x1, waiting for transfers between devices, shards(): lax.psum_scatter(jnp.einsum('al,ikra->ikrl', analysis, pair_values, prefe...  36.4 us
    slice x15, local copies, waits for them, and re-layouts, line_sums(): forward_blocks[:, :, :, :block_size - distance]  36.3 us
    add x2, other arithmetic, line_sums(): backward + factor * jnp.concatenate([backward_blocks[:, :, :, distance:],...  36.2 us
    all_gather x1, waiting for transfers between devices, shards(): lax.all_gather(radial_potential, 'orb', axis=0, tiled=True)  35.6 us
    reduce_scatter x1, waiting for transfers between devices, shards(): lax.psum_scatter(jnp.einsum('al,kra->lkr', analysis, product, preferred_e...  34.9 us
  transfers between devices with their start and end apart: 4, of which 4 were waited for; matrix products, arithmetic and copies ran while one was open for 1% of the time, Pallas kernels for 0%

commit v1 on v0

--- a/solution.py
+++ b/solution.py
@@ -116,7 +116,11 @@
         line_density.astype(jnp.float32), degree, points
     )
     potential = finish_potential(forward, backward, radius, scaled, degree).astype(jnp.bfloat16)
-    radial_potential = lax.all_to_all(potential, "grid", split_axis=2, concat_axis=3, tiled=True)
+    wide_out = jnp.split(potential, lax.axis_size("grid"), axis=2)
+    built = jnp.stack(wide_out)
+    radial_potential = jnp.concatenate(
+        lax.all_to_all(built, axis_name="grid", split_axis=0, concat_axis=0), axis=3
+    )
     pot_ang = jnp.einsum(
         "al,ikrl->ikra",
         harmonic_table,

time: 543 us -> 542 us (level)
    unnamed x179 -> x194, local copies, waits for them, and re-layouts: 69.2 us -> 69.4 us
where the time goes in v1:
time: 542 us; the launch traced here: 536 us
  local copies, waits for them, and re-layouts  178 us (33%)
  waiting for transfers between devices  128 us (24%)
  other arithmetic  118 us (22%)
  blocking collectives  65.8 us (12%)
  matrix products  24.2 us (4%)
  between operations  15 us (3%)
  starting transfers between devices  5.71 us (1%)
    unnamed x194, local copies, waits for them, and re-layouts  69.4 us
    all_to_all x1, blocking collectives, shards(): lax.all_to_all(built, axis_name='grid', split_axis=0, concat_axis=0)  54.8 us
    add x1, other arithmetic, line_sums(): forward + factor * jnp.concatenate([padding, forward_blocks[:, :, :, :blo...  43.8 us
    reduce_scatter x1, waiting for transfers between devices, shards(): lax.psum_scatter(jnp.einsum('al,ikra->ikrl', analysis, pair_values, prefe...  36.4 us
    slice x15, local copies, waits for them, and re-layouts, line_sums(): forward_blocks[:, :, :, :block_size - distance]  36.3 us
    add x2, other arithmetic, line_sums(): backward + factor * jnp.concatenate([backward_blocks[:, :, :, distance:],...  36.2 us
    all_gather x1, waiting for transfers between devices, shards(): lax.all_gather(radial_potential, 'orb', axis=0, tiled=True)  35.6 us
    reduce_scatter x1, waiting for transfers between devices, shards(): lax.psum_scatter(jnp.einsum('al,kra->lkr', analysis, product, preferred_e...  34.9 us
  transfers between devices with their start and end apart: 4, of which 4 were waited for; matrix products, arithmetic and copies ran while one was open for 1% of the time, Pallas kernels for 0%

profile of v1, /device:TPU:0, one launch (start us, length us, event | category | flops | bytes accessed | tf_op | source)
XLA Modules:
  0.0 535.7 jit_solution(16486263948692369538)
XLA Ops:
  6.5 11.0 %all_gather.6 = bf16[2,64,2304]{2,1,0:T(8,128)(2,1)S(1)} all-gather(bf16[1,64,2304]{2,1,0:T(8,128)(2,1)} %param.5), channel_id=1, replica_groups=mesh['orb'=2,'grid'=16] {'orb'}, dimensions={0}, use_global_device_ids=true | all-gather | bytes 884736 | tf_op jit(solution)/shard_map/all_gather | solution.py:91
  17.5 4.8 fusion.27
  24.1 5.0 fusion.10
  29.2 36.4 %reduce-scatter.3.cloned.1.call-done = bf16[1,4,64,2304]{3,2,1,0:T(8,128)(2,1)} async-done(((bf16[2,4,64,2304]{3,2,1,0:T(8,128)(2,1)}), bf16[1,4,64,2304]{3,2,1,0:T(8,128)(2,1)}) %reduce-scatter.3.cloned.1.call-update) | async-done | bytes 1179664 | tf_op jit(solution)/shard_map/reduce_scatter | solution.py:100
  65.5 4.2 copy.101
  72.2 5.6 %all-to-all-start = ((bf16[16,2,18432]{2,1,0:T(2,128)(2,1)}), bf16[16,2,18432]{2,1,0:T(2,128)(2,1)S(1)}, u32[]{:S(2)}, u32[]{:S(2)}) async-start(bf16[16,2,18432]{2,1,0:T(2,128)(2,1)} %reshape.327), calls=%async_computation.1 | async-start | bytes 2359296 | tf_op jit(solution)/shard_map/all_to_all | solution.py:113
  81.4 21.5 %all-to-all-done = bf16[16,2,18432]{2,1,0:T(2,128)(2,1)S(1)} async-done(((bf16[16,2,18432]{2,1,0:T(2,128)(2,1)}), bf16[16,2,18432]{2,1,0:T(2,128)(2,1)S(1)}, u32[]{:S(2)}, u32[]{:S(2)}) %all-to-all-start) | async-done | bytes 1179680 | tf_op jit(solution)/shard_map/all_to_all | solution.py:113
  104.5 5.4 %copy.128 = f32[1,4,64,16,144]{4,2,3,1,0:T(8,128)} copy(bf16[1,4,64,16,144]{2,1,4,3,0:T(4,128)(2,1)S(1)} %bitcast.138) | data formatting | bytes 3538944 | tf_op jit(solution)/shard_map/convert_element_type | solution.py:116
  109.8 7.8 %copy_multiply_fusion = f32[1,4,64,16,144]{4,0,3,2,1:T(1,128)S(1)} fusion(f32[1,4,64,16,144]{4,3,2,1,0:T(8,128)} %bitcast.135, f32[64,16]{1,0:T(8,128)S(1)} %copy-done.29), kind=kLoop, calls=%fused_computation.17 | loop fusion | flops 589824 | bytes 4722688 | tf_op jit(solution)/shard_map/mul | solution.py:73
  117.7 5.5 %slice.492 = f32[1,4,64,15,144]{4,0,3,2,1:T(1,128)} slice(f32[1,4,64,16,144]{4,0,3,2,1:T(1,128)S(1)} %copy_multiply_fusion), slice={[0:1], [0:4], [0:64], [0:15], [0:144]} | slice | bytes 4423680 | tf_op jit(solution)/shard_map/slice | solution.py:36
  123.1 5.2 slice.493
  128.4 3.1 slice.494
  131.4 3.0 slice.495
  134.5 2.6 slice.496
  143.5 3.2 slice.500
  146.7 2.6 slice.501
  154.5 43.8 %multiply_add_fusion.3 = f32[1,4,64,16,144]{4,0,3,2,1:T(1,128)S(1)} fusion(f32[1,4,64,1,144]{4,0,3,2,1:T(1,128)S(1)} %slice.506, f32[1,4,64,2,144]{4,0,3,2,1:T(1,128)S(1)} %slice.505, f32[1,4,64,3,144]{4,0,3,2,1:T(1,128)S(1)} %slice.504, f32[1,4,64,4,144]{4,0,3,2,1:T(1,128)S(1)} %slice.503, f32[1,4,64,5,144]{4,0,3,2,1:T(1,128)} %slice.502, ...), kind=kLoop, calls=%fused_computation.21 | loop fusion | flops 18284544 | bytes 22426048 | tf_op jit(solution)/shard_map/add | solution.py:35
  206.0 2.7 broadcast_multiply_fusion.1
  208.7 3.0 slice.526
  211.7 2.6 slice.527
  214.3 2.7 slice.528
  217.0 2.6 slice.529
  219.6 2.6 slice.530
  222.2 2.6 slice.531
  224.8 2.7 slice.532
  235.9 8.1 %copy.152 = f32[1,4,64,15,144]{4,0,3,2,1:T(1,128)} copy(f32[1,4,64,15,144]{4,3,2,1,0:T(8,128)} %slice.526) | data formatting | bytes 4423680
  244.0 8.1 %copy.151 = f32[1,4,64,14,144]{4,0,3,2,1:T(1,128)} copy(f32[1,4,64,14,144]{4,3,2,1,0:T(8,128)} %slice.527) | data formatting | bytes 4128768
  252.2 5.4 %copy.150 = f32[1,4,64,13,144]{4,0,3,2,1:T(1,128)} copy(f32[1,4,64,13,144]{4,3,2,1,0:T(8,128)S(1)} %copy-done.10) | data formatting | bytes 3833856
  257.6 3.3 copy.149
  260.9 4.8 copy.148
  265.7 2.8 copy.147
  268.5 2.5 copy.146
  273.2 4.8 copy.144
  278.1 3.2 copy.143
  281.4 3.1 copy.142
  288.4 35.6 %multiply_add_fusion.1 = f32[1,4,64,16,144]{4,0,3,2,1:T(1,128)S(1)} fusion(f32[1,4,64,2,144]{4,0,3,2,1:T(1,128)S(1)} %copy.139, f32[1,4,64,3,144]{4,0,3,2,1:T(1,128)S(1)} %copy.140, f32[1,4,64,4,144]{4,0,3,2,1:T(1,128)S(1)} %copy.141, f32[1,4,64,5,144]{4,0,3,2,1:T(1,128)S(1)} %copy.142, f32[1,4,64,6,144]{4,0,3,2,1:T(1,128)} %copy.143, ...), kind=kLoop, calls=%fused_computation.19 | loop fusion | flops 16515072 | bytes 22273920 | tf_op jit(solution)/shard_map/add | solution.py:38
  331.0 10.6 %pad.124 = f32[1,4,16,144]{3,0,2,1:T(1,128)S(1)} pad(f32[1,4,8,144]{3,0,2,1:T(1,128)} %pad_maximum_fusion.5, f32[]{:T(128)} %constant.31.clone.1), padding=0_0_0x0_0_0x0_1_1x0_0_0 | pad | bytes 55300 | tf_op jit(solution)/shard_map/pad | solution.py:47
  342.5 3.0 broadcast_multiply_fusion
  349.5 9.2 %multiply_add_fusion.2 = f32[1,4,64,16,144]{4,0,3,2,1:T(1,128)} fusion(f32[1,4,64,16,144]{4,0,3,2,1:T(1,128)} %copy-done.6, f32[4,64,144]{2,1,0:T(8,128)S(1)} %pad_bitcast_fusion.1, f32[16,144]{1,0:T(8,128)S(1)} %copy-done.31), kind=kLoop, calls=%fused_computation.20 | loop fusion | flops 1179648 | bytes 4875264 | tf_op jit(solution)/shard_map/add | solution.py:54
  358.7 4.7 copy.132
  369.5 7.0 %copy.130 = f32[1,4,64,16,144]{4,2,3,1,0:T(8,128)} copy(f32[1,4,64,16,144]{2,1,4,3,0:T(4,128)} %bitcast.139) | data formatting | bytes 4718592 | tf_op jit(solution)/shard_map/mul | solution.py:74
  376.5 3.1 multiply_add_fusion
  383.1 54.8 %all_to_all.14 = bf16[16,1,4,64,144]{4,3,2,1,0:T(8,128)(2,1)S(1)} all-to-all(bf16[16,1,4,64,144]{4,3,2,1,0:T(8,128)(2,1)S(1)} %fusion.37), channel_id=1, replica_groups=mesh['orb'=2,'grid'=16] {'grid'}, dimensions={0} | all-to-all | bytes 2359296 | tf_op jit(solution)/shard_map/all_to_all | solution.py:122
  439.2 4.1 reshape.320
  443.3 35.6 %all-gather.2.cloned.1.call-done = bf16[2,4,64,2304]{3,2,1,0:T(8,128)(2,1)} async-done(((bf16[1,4,64,2304]{3,2,1,0:T(8,128)(2,1)}), bf16[2,4,64,2304]{3,2,1,0:T(8,128)(2,1)}) %all-gather.2.cloned.1.call-update) | async-done | bytes 2359312 | tf_op jit(solution)/shard_map/all_gather | solution.py:127
  479.0 6.7 %fusion.30 = bf16[4,64,1280]{2,1,0:T(8,128)(2,1)S(1)} fusion(bf16[2,4,64,2304]{3,2,1,0:T(8,128)(2,1)} %all-gather.2.cloned.1.call-done, bf16[1280,2304]{1,0:T(8,128)(2,1)} %param.7, f32[2,64,1280]{2,1,0:T(8,128)S(1)} %copy-done.27), kind=kOutput, calls=%fused_computation.30 | convolution fusion | flops 3020881920 | bytes 9568256 | tf_op jit(solution)/shard_map/al,ikrl->ikra/dot_general | solution.py:124
  485.7 6.0 %fusion.8 = f32[2304,4,64]{0,2,1:T(8,128)} fusion(bf16[1280,2304]{1,0:T(8,128)(2,1)} %param.7, f32[1280]{0:T(1024)S(1)} %copy-done.75, bf16[4,64,1280]{2,1,0:T(8,128)(2,1)S(1)} %fusion.30), kind=kOutput, calls=%fused_computation.9 | convolution fusion | flops 1518796800 | bytes 8918016 | tf_op jit(solution)/shard_map/al,kra->lkr/dot_general | solution.py:133
  491.7 34.9 %reduce-scatter.5.cloned.1.call-done = f32[1152,4,64]{0,2,1:T(8,128)} async-done(((f32[2304,4,64]{0,2,1:T(8,128)}), f32[1152,4,64]{0,2,1:T(8,128)}) %reduce-scatter.5.cloned.1.call-update) | async-done | bytes 1179664 | tf_op jit(solution)/shard_map/reduce_scatter | solution.py:132
  (300 shorter events, 67.1 us)
Async XLA Ops:
  6.5 15.8 %copy-start = (bf16[4,64,2304]{2,1,0:T(8,128)(2,1)S(1)}, bf16[4,64,2304]{2,1,0:T(8,128)(2,1)}, u32[]{:S(2)}) copy-start(bf16[4,64,2304]{2,1,0:T(8,128)(2,1)} %param.6) | copy-start | bytes 3538948
  6.5 59.0 %reduce-scatter.3.cloned.1.call-start = ((), (), s32[]{:S(2)}) async-start(), calls=%async_computation.4 | async-start | bytes 3538944 | tf_op jit(solution)/shard_map/reduce_scatter | solution.py:100
  6.5 15.8 %slice-start.1 = ((s8[5898240]{0:T(1024)(128)(4,1)}), s8[4194304]{0:T(1024)(128)(4,1)S(1)}, s32[]{:S(2)}) async-start(s8[5898240]{0:T(1024)(128)(4,1)} %bitcast.141), calls=%async_computation.8 | async-start | bytes 8388608
  72.2 30.8 %all-to-all-start = ((bf16[16,2,18432]{2,1,0:T(2,128)(2,1)}), bf16[16,2,18432]{2,1,0:T(2,128)(2,1)S(1)}, u32[]{:S(2)}, u32[]{:S(2)}) async-start(bf16[16,2,18432]{2,1,0:T(2,128)(2,1)} %reshape.327), calls=%async_computation.1 | async-start | bytes 2359296 | tf_op jit(solution)/shard_map/all_to_all | solution.py:113
  77.8 401.2 %all-gather.2.cloned.1.call-start = ((), (), s32[]{:S(2)}) async-start(), calls=%async_computation.5 | async-start | bytes 3538944 | tf_op jit(solution)/shard_map/all_gather | solution.py:127
  143.5 10.7 %copy-start.16 = (f32[1,4,64,14,144]{4,0,3,2,1:T(1,128)S(1)}, f32[1,4,64,14,144]{4,0,3,2,1:T(1,128)}, u32[]{:S(2)}) copy-start(f32[1,4,64,14,144]{4,0,3,2,1:T(1,128)} %slice.493) | copy-start | bytes 6193156
  146.7 7.5 %copy-start.15 = (f32[1,4,64,15,144]{4,0,3,2,1:T(1,128)S(1)}, f32[1,4,64,15,144]{4,0,3,2,1:T(1,128)}, u32[]{:S(2)}) copy-start(f32[1,4,64,15,144]{4,0,3,2,1:T(1,128)} %slice.492) | copy-start | bytes 6635524
  154.4 46.2 %copy-start.32 = (f32[144]{0:T(256)S(1)}, f32[144]{0:T(256)}, u32[]{:S(2)}) copy-start(f32[144]{0:T(256)} %get-tuple-element.42) | copy-start | bytes 1732
  154.4 46.3 %copy-start.68 = (f32[144]{0:T(256)S(1)}, f32[144]{0:T(256)}, u32[]{:S(2)}) copy-start(f32[144]{0:T(256)} %get-tuple-element.43) | copy-start | bytes 1732
  154.4 46.4 %copy-start.69 = (f32[144]{0:T(256)S(1)}, f32[144]{0:T(256)}, u32[]{:S(2)}) copy-start(f32[144]{0:T(256)} %get-tuple-element.47) | copy-start | bytes 1732
  154.4 46.5 %copy-start.70 = (f32[144]{0:T(256)S(1)}, f32[144]{0:T(256)}, u32[]{:S(2)}) copy-start(f32[144]{0:T(256)} %get-tuple-element.46) | copy-start | bytes 1732
  154.4 46.5 %copy-start.71 = (f32[144]{0:T(256)S(1)}, f32[144]{0:T(256)}, u32[]{:S(2)}) copy-start(f32[144]{0:T(256)} %get-tuple-element.44) | copy-start | bytes 1732
  154.4 46.5 %copy-start.73 = (f32[144]{0:T(256)S(1)}, f32[144]{0:T(256)}, u32[]{:S(2)}) copy-start(f32[144]{0:T(256)} %get-tuple-element.45) | copy-start | bytes 1732
  200.6 8.1 %copy-start.25 = (f32[1,4,64,144]{3,0,2,1:T(1,128)}, f32[1,4,64,144]{3,0,2,1:T(1,128)S(1)}, u32[]{:S(2)}) copy-start(f32[1,4,64,144]{3,0,2,1:T(1,128)S(1)} %slice_bitcast_fusion.1) | copy-start | bytes 442372
  208.7 26.2 %copy-start.2 = (f32[1,4,64,16,144]{4,3,2,1,0:T(8,128)}, f32[1,4,64,16,144]{4,3,2,1,0:T(8,128)S(1)}, u32[]{:S(2)}) copy-start(f32[1,4,64,16,144]{4,3,2,1,0:T(8,128)S(1)} %broadcast_multiply_fusion.1) | copy-start | bytes 7077892
  244.0 8.1 %copy-start.10 = (f32[1,4,64,13,144]{4,3,2,1,0:T(8,128)S(1)}, f32[1,4,64,13,144]{4,3,2,1,0:T(8,128)}, u32[]{:S(2)}) copy-start(f32[1,4,64,13,144]{4,3,2,1,0:T(8,128)} %slice.528) | copy-start | bytes 5750788
  268.5 9.6 %copy-start.20 = (f32[1,4,64,6,144]{4,3,2,1,0:T(8,128)S(1)}, f32[1,4,64,6,144]{4,3,2,1,0:T(8,128)}, u32[]{:S(2)}) copy-start(f32[1,4,64,6,144]{4,3,2,1,0:T(8,128)} %slice.535) | copy-start | bytes 2654212
  271.0 17.1 %copy-start.19 = (f32[1,4,64,11,144]{4,0,3,2,1:T(1,128)S(1)}, f32[1,4,64,11,144]{4,0,3,2,1:T(1,128)}, u32[]{:S(2)}) copy-start(f32[1,4,64,11,144]{4,0,3,2,1:T(1,128)} %copy.148) | copy-start | bytes 4866052
  273.2 14.4 %copy-start.23 = (f32[1,4,64,2,144]{4,3,2,1,0:T(2,128)S(1)}, f32[1,4,64,2,144]{4,3,2,1,0:T(2,128)}, u32[]{:S(2)}) copy-start(f32[1,4,64,2,144]{4,3,2,1,0:T(2,128)} %slice.539) | copy-start | bytes 884740
  273.2 15.0 %copy-start.18 = (f32[1,4,64,13,144]{4,0,3,2,1:T(1,128)S(1)}, f32[1,4,64,13,144]{4,0,3,2,1:T(1,128)}, u32[]{:S(2)}) copy-start(f32[1,4,64,13,144]{4,0,3,2,1:T(1,128)} %copy.150) | copy-start | bytes 5750788
  278.1 10.1 %copy-start.17 = (f32[1,4,64,14,144]{4,0,3,2,1:T(1,128)S(1)}, f32[1,4,64,14,144]{4,0,3,2,1:T(1,128)}, u32[]{:S(2)}) copy-start(f32[1,4,64,14,144]{4,0,3,2,1:T(1,128)} %copy.151) | copy-start | bytes 6193156
  281.3 6.9 %copy-start.14 = (f32[1,4,64,15,144]{4,0,3,2,1:T(1,128)S(1)}, f32[1,4,64,15,144]{4,0,3,2,1:T(1,128)}, u32[]{:S(2)}) copy-start(f32[1,4,64,15,144]{4,0,3,2,1:T(1,128)} %copy.152) | copy-start | bytes 6635524
  281.3 7.0 %copy-start.41 = (f32[144]{0:T(256)S(1)}, f32[144]{0:T(256)}, u32[]{:S(2)}) copy-start(f32[144]{0:T(256)} %get-tuple-element.27) | copy-start | bytes 1732
  281.3 7.0 %copy-start.43 = (f32[144]{0:T(256)S(1)}, f32[144]{0:T(256)}, u32[]{:S(2)}) copy-start(f32[144]{0:T(256)} %get-tuple-element.28) | copy-start | bytes 1732
  281.3 7.0 %copy-start.45 = (f32[144]{0:T(256)S(1)}, f32[144]{0:T(256)}, u32[]{:S(2)}) copy-start(f32[144]{0:T(256)} %get-tuple-element.29) | copy-start | bytes 1732
  281.3 7.0 %copy-start.47 = (f32[144]{0:T(256)S(1)}, f32[144]{0:T(256)}, u32[]{:S(2)}) copy-start(f32[144]{0:T(256)} %get-tuple-element.30) | copy-start | bytes 1732
  281.3 7.0 %copy-start.49 = (f32[144]{0:T(256)S(1)}, f32[144]{0:T(256)}, u32[]{:S(2)}) copy-start(f32[144]{0:T(256)} %get-tuple-element.31) | copy-start | bytes 1732
  281.3 7.0 %copy-start.51 = (f32[144]{0:T(256)S(1)}, f32[144]{0:T(256)}, u32[]{:S(2)}) copy-start(f32[144]{0:T(256)} %get-tuple-element.32) | copy-start | bytes 1732
  281.3 7.0 %copy-start.53 = (f32[144]{0:T(256)S(1)}, f32[144]{0:T(256)}, u32[]{:S(2)}) copy-start(f32[144]{0:T(256)} %get-tuple-element.33) | copy-start | bytes 1732
  281.3 7.0 %copy-start.55 = (f32[144]{0:T(256)S(1)}, f32[144]{0:T(256)}, u32[]{:S(2)}) copy-start(f32[144]{0:T(256)} %get-tuple-element.34) | copy-start | bytes 1732
  281.3 7.0 %copy-start.57 = (f32[144]{0:T(256)S(1)}, f32[144]{0:T(256)}, u32[]{:S(2)}) copy-start(f32[144]{0:T(256)} %get-tuple-element.35) | copy-start | bytes 1732
  281.3 7.0 %copy-start.59 = (f32[144]{0:T(256)S(1)}, f32[144]{0:T(256)}, u32[]{:S(2)}) copy-start(f32[144]{0:T(256)} %get-tuple-element.36) | copy-start | bytes 1732
  281.3 7.0 %copy-start.61 = (f32[144]{0:T(256)S(1)}, f32[144]{0:T(256)}, u32[]{:S(2)}) copy-start(f32[144]{0:T(256)} %get-tuple-element.37) | copy-start | bytes 1732
  281.4 7.0 %copy-start.63 = (f32[144]{0:T(256)S(1)}, f32[144]{0:T(256)}, u32[]{:S(2)}) copy-start(f32[144]{0:T(256)} %get-tuple-element.38) | copy-start | bytes 1732
  281.4 7.0 %copy-start.65 = (f32[144]{0:T(256)S(1)}, f32[144]{0:T(256)}, u32[]{:S(2)}) copy-start(f32[144]{0:T(256)} %get-tuple-element.39) | copy-start | bytes 1732
  281.4 7.0 %copy-start.67 = (f32[144]{0:T(256)S(1)}, f32[144]{0:T(256)}, u32[]{:S(2)}) copy-start(f32[144]{0:T(256)} %get-tuple-element.40) | copy-start | bytes 1732
  288.4 35.6 %copy-start.22 = (f32[1,4,64,1,144]{4,3,2,1,0:T(1,128)S(1)}, f32[1,4,64,1,144]{4,3,2,1,0:T(1,128)}, u32[]{:S(2)}) copy-start(f32[1,4,64,1,144]{4,3,2,1,0:T(1,128)} %slice.540) | copy-start | bytes 442372
  288.4 35.6 %copy-start.36 = (f32[144]{0:T(256)S(1)}, f32[144]{0:T(256)}, u32[]{:S(2)}) copy-start(f32[144]{0:T(256)} %get-tuple-element.41) | copy-start | bytes 1732
  326.3 19.3 %copy-start.24 = (f32[1,4,64,144]{3,0,2,1:T(1,128)}, f32[1,4,64,144]{3,0,2,1:T(1,128)S(1)}, u32[]{:S(2)}) copy-start(f32[1,4,64,144]{3,0,2,1:T(1,128)S(1)} %slice_bitcast_fusion) | copy-start | bytes 442372
  329.6 17.6 %slice-start.4 = ((f32[1,4,64,144]{3,0,2,1:T(1,128)}), f32[1,4,1,144]{3,0,2,1:T(1,128)S(1)}, s32[]{:S(2)}) async-start(f32[1,4,64,144]{3,0,2,1:T(1,128)} %copy-done.25), calls=%async_computation.11 | async-start | bytes 8192 | tf_op jit(solution)/shard_map/slice | solution.py:44
  329.6 17.6 %copy-start.28 = (f32[1,4,31,144]{3,0,2,1:T(1,128)S(1)}, f32[1,4,31,144]{3,0,2,1:T(1,128)}, u32[]{:S(2)}) copy-start(f32[1,4,31,144]{3,0,2,1:T(1,128)} %fusion.54) | copy-start | bytes 214276
  358.7 8.2 %copy-start.34 = (f32[144]{0:T(256)S(1)}, f32[144]{0:T(256)}, u32[]{:S(2)}) copy-start(f32[144]{0:T(256)} %get-tuple-element.42) | copy-start | bytes 1732
  358.7 8.5 %slice-start.3 = ((f32[1,4,64,144]{3,0,2,1:T(1,128)}), f32[1,4,1,144]{3,0,2,1:T(1,128)S(1)}, s32[]{:S(2)}) async-start(f32[1,4,64,144]{3,0,2,1:T(1,128)} %copy-done.24), calls=%async_computation.10 | async-start | bytes 8192 | tf_op jit(solution)/shard_map/slice | solution.py:47
  369.5 7.0 %copy-start.37 = (f32[144]{0:T(256)S(1)}, f32[144]{0:T(256)}, u32[]{:S(2)}) copy-start(f32[144]{0:T(256)} %get-tuple-element.41) | copy-start | bytes 1732
  437.9 41.0 %copy-start.27 = (f32[2,64,1280]{2,1,0:T(8,128)S(1)}, f32[2,64,1280]{2,1,0:T(8,128)}, u32[]{:S(2)}) copy-start(f32[2,64,1280]{2,1,0:T(8,128)} %copy-done.26) | copy-start | bytes 1966084
  443.3 42.4 %copy-start.75 = (f32[1280]{0:T(1024)S(1)}, f32[1280]{0:T(1024)}, u32[]{:S(2)}) copy-start(f32[1280]{0:T(1024)} %param.8) | copy-start | bytes 15364
  443.3 83.3 %reduce-scatter.5.cloned.1.call-start = ((), (), s32[]{:S(2)}) async-start(), calls=%async_computation.6 | async-start | bytes 3538944 | tf_op jit(solution)/shard_map/reduce_scatter | solution.py:132
  485.7 43.3 %copy-start.1 = (bf16[4,64,2304]{2,1,0:T(8,128)(2,1)S(1)}, bf16[4,64,2304]{2,1,0:T(8,128)(2,1)}, u32[]{:S(2)}) copy-start(bf16[4,64,2304]{2,1,0:T(8,128)(2,1)} %param.6) | copy-start | bytes 3538948
  (37 other events, 162.1 us)
Sparse Core Ops, SparseCore 0:
  29.3 36.1 reduce-scatter.2
  443.4 35.5 all-gather.1
  491.8 34.6 reduce-scatter.4
